TPU v7x, 32 devices: a whole 2x2x4 slice. The times are simulated.
32 devices in a mesh: dp: 4 (over y, x), expert: 8 (over z, core).
Axes of the slice: x: 2, y: 2, z: 4, core: 2. Of those that a mesh axis runs over, the one named last changes fastest.
Arguments:
- tokens: bfloat16 [1024, 2048], P(('dp', 'expert')), may hold values from -6 to 6
- grad_out: bfloat16 [1024, 2048], P(('dp', 'expert')), may hold values from -0.59765625 to 0.59765625
- routing: int32 [1024, 8], P(('dp', 'expert')), may hold values from 0 to 15, as said below
- replica: int32 [1024, 8], P(('dp', 'expert')), may hold values from 0 to 1, as said below
- gates: bfloat16 [1024, 8], P(('dp', 'expert')), may hold values from 0.25 to 4
- host_expert: int32 [8], replicated, may hold values from 0 to 15, as said below
- w_gate_up: bfloat16 [16, 2, 768, 2048], P('expert', None, 'dp'), may hold values from -0.125 to 0.125
- w_down: bfloat16 [16, 768, 2048], P('expert', 'dp'), may hold values from -0.21875 to 0.21875
Outputs:
- grad_tokens: bfloat16 [1024, 2048], P(('dp', 'expert'))
- grad_gates: float32 [1024, 8], P(('dp', 'expert'))
- grad_w_gate_up: bfloat16 [16, 2, 768, 2048], P('expert', None, 'dp')
- grad_w_down: bfloat16 [16, 768, 2048], P('expert', 'dp')
Inputs may be any that keep to these rules, and one draw needn't show every extreme that they name: `routing`: column k of a token names an expert of 2 * k to 2 * k + 1. Within the rows of one device, experts 2 i and 2 i + 1 are named together exactly 2 * 16 times. `replica`: within the rows of one device, each expert has at most 16 choices marked 0 and at most 16 marked 1; some expert reaches 16 marked 0 from every device, and in every index of dp some expert reaches 16 marked 1 from every device. Only experts listed in host_expert have choices marked 1. `host_expert`: for every device d of the expert axis exactly one of its experts 2 d and 2 d + 1 is listed, and it is listed once.
All inputs are finite; a program needn't handle non-finite values.
Results may differ from a plain program's by a relative error of at most 0.013.
Values may be sent and summed in bfloat16 or wider, within the bound.
A program may use at most 128 MiB of HBM per device.

v0:
```python
import jax
import jax.numpy as jnp
from jax import lax
from jax.sharding import PartitionSpec as P


def lookup(values_table, indices):
    matches = indices[..., None] == lax.broadcasted_iota(
        jnp.int32, indices.shape + values_table.shape, indices.ndim
    )
    return jnp.sum(jnp.where(matches, values_table, 0), axis=-1)


def placement(host_expert, owned_experts, devices):
    experts = owned_experts * devices
    matches = host_expert[None, :] == lax.broadcasted_iota(jnp.int32, (experts, devices), 0)
    helper_ids = lax.broadcasted_iota(jnp.int32, (experts, devices), 1)
    helper_of = jnp.sum(jnp.where(matches, helper_ids, 0), axis=1)
    listed = jnp.sum(matches.astype(jnp.int32), axis=1)
    return (helper_of, listed)


def targets(routing, replica, host_expert, owned_experts, devices, slot_rows, groups):
    helper_of, listed = placement(host_expert, owned_experts, devices)
    choices = routing.shape[0] // groups * routing.shape[1]
    usable = (replica == 0) | (lookup(listed, routing) > 0)
    device_to = jnp.where(replica == 0, routing // owned_experts, lookup(helper_of, routing))
    block_to = jnp.where(replica == 0, routing % owned_experts, owned_experts)
    labels = (routing * 2 + replica).reshape(groups, choices)
    earlier = lax.broadcasted_iota(jnp.int32, (choices, choices), 1) < lax.broadcasted_iota(
        jnp.int32, (choices, choices), 0
    )
    matching = (labels[:, :, None] == labels[:, None, :]) & earlier[None]
    ranking = jnp.sum(matching.astype(jnp.int32), axis=2).reshape(routing.shape)
    group_ids = lax.broadcasted_iota(jnp.int32, (groups, choices), 0).reshape(routing.shape)
    position = ((block_to * groups + group_ids) * devices + device_to) * slot_rows + ranking
    return jnp.where(usable, position, -1)


def selector(position, total_slots):
    matches = position[None, :, :] == lax.broadcasted_iota(
        jnp.int32, (total_slots,) + position.shape, 0
    )
    picker = jnp.sum(matches.astype(jnp.float32), axis=2).astype(jnp.bfloat16)
    return (matches, picker)


def fill_rows(matches, picker, tokens, grad_out, gates):
    row_x = jnp.dot(picker, tokens, preferred_element_type=jnp.float32).astype(jnp.bfloat16)
    row_dy = jnp.dot(picker, grad_out, preferred_element_type=jnp.float32).astype(jnp.bfloat16)
    row_gate = jnp.sum(
        jnp.where(matches, gates[None].astype(jnp.float32), 0.0), axis=(1, 2)
    ).astype(jnp.bfloat16)
    return (row_x, row_dy, row_gate)


def expert_block(inputs, upstream, weight, gate_up, down_matrix):
    mixed = jnp.einsum("rd,jfd->jrf", inputs, gate_up, preferred_element_type=jnp.float32)
    gate_pre = mixed[0]
    up_part = mixed[1]
    sigmoid_gate = jax.nn.sigmoid(gate_pre)
    active = gate_pre * sigmoid_gate
    hidden = (active * up_part).astype(jnp.bfloat16)
    output_part = jnp.einsum("rf,fd->rd", hidden, down_matrix, preferred_element_type=jnp.float32)
    gate_part = jnp.sum(output_part * upstream.astype(jnp.float32), axis=1)
    scaled = (weight.astype(jnp.float32)[:, None] * upstream.astype(jnp.float32)).astype(
        jnp.bfloat16
    )
    grad_hidden = jnp.einsum("rd,fd->rf", scaled, down_matrix, preferred_element_type=jnp.float32)
    grad_gate = grad_hidden * up_part * sigmoid_gate * (1.0 + gate_pre * (1.0 - sigmoid_gate))
    grad_mixed = jnp.stack([grad_gate, grad_hidden * active], axis=0).astype(jnp.bfloat16)
    input_part = jnp.einsum("jrf,jfd->rd", grad_mixed, gate_up, preferred_element_type=jnp.float32)
    weight_gu = jnp.einsum("jrf,rd->jfd", grad_mixed, inputs, preferred_element_type=jnp.float32)
    weight_down = jnp.einsum("rf,rd->fd", hidden, scaled, preferred_element_type=jnp.float32)
    return (input_part, gate_part, weight_gu, weight_down)


def shards(tokens, grad_out, routing, replica, gates, host_expert, w_gate_up, w_down):
    devices = lax.axis_size("expert")
    device_id = lax.axis_index("expert")
    token_rows, features = tokens.shape
    owned_experts = w_gate_up.shape[0]
    quarter = w_down.shape[1]
    topk_width = routing.shape[1]
    slot_rows = token_rows * topk_width // (owned_experts * devices)
    blocks = owned_experts + 1
    lane_rows = devices * slot_rows
    piece_rows = quarter // devices
    home_slots = targets(routing, replica, host_expert, owned_experts, devices, slot_rows, 1)
    home_matches, home_picker = selector(home_slots, blocks * lane_rows)
    row_x, row_dy, row_gate = fill_rows(home_matches, home_picker, tokens, grad_out, gates)
    sent_x, sent_dy, sent_gate = (
        lax.all_to_all(
            row_x.reshape(blocks, lane_rows, features),
            "expert",
            split_axis=1,
            concat_axis=1,
            tiled=True,
        ),
        lax.all_to_all(
            row_dy.reshape(blocks, lane_rows, features),
            "expert",
            split_axis=1,
            concat_axis=1,
            tiled=True,
        ),
        lax.all_to_all(
            row_gate.reshape(blocks, lane_rows), "expert", split_axis=1, concat_axis=1, tiled=True
        ),
    )
    block_x, block_dy, block_gate = (
        lax.all_gather(sent_x, "dp", axis=1, tiled=True),
        lax.all_gather(sent_dy, "dp", axis=1, tiled=True),
        lax.all_gather(sent_gate, "dp", axis=1, tiled=True),
    )
    owner_of_helper = host_expert // owned_experts
    owns_copy = owner_of_helper == device_id
    copied_local = jnp.sum(jnp.where(owns_copy, host_expert % owned_experts, 0))
    helper_ids = lax.broadcasted_iota(jnp.int32, (devices, devices), 1)
    owner_ids = lax.broadcasted_iota(jnp.int32, (devices, devices), 0)
    helper_of_owner = jnp.sum(
        jnp.where(owner_of_helper[None, :] == owner_ids, helper_ids, 0), axis=1
    )
    source_gu = lax.dynamic_index_in_dim(w_gate_up, copied_local, 0, keepdims=False)
    source_down = lax.dynamic_index_in_dim(w_down, copied_local, 0, keepdims=False)
    spread_gu, spread_down = (
        lax.all_to_all(
            source_gu.reshape(2, devices, piece_rows, features),
            "expert",
            split_axis=1,
            concat_axis=1,
            tiled=True,
        ),
        lax.all_to_all(
            source_down.reshape(1, devices, piece_rows, features),
            "expert",
            split_axis=1,
            concat_axis=1,
            tiled=True,
        ),
    )
    spread_gu = jnp.take(spread_gu, owner_of_helper, axis=1)
    spread_down = jnp.take(spread_down, owner_of_helper, axis=1)
    hosted_gu, hosted_down = (
        lax.all_to_all(spread_gu, "expert", split_axis=1, concat_axis=1, tiled=True),
        lax.all_to_all(spread_down, "expert", split_axis=1, concat_axis=1, tiled=True),
    )
    hosted_gu = hosted_gu.reshape(2, quarter, features)
    hosted_down = hosted_down.reshape(quarter, features)
    input_parts = []
    gate_parts = []
    owner_gu = []
    owner_down = []
    for block in range(blocks):
        if block < owned_experts:
            gate_up = w_gate_up[block]
            down_matrix = w_down[block]
        else:
            gate_up = hosted_gu
            down_matrix = hosted_down
        input_part, gate_part, weight_gu, weight_down = expert_block(
            block_x[block], block_dy[block], block_gate[block], gate_up, down_matrix
        )
        input_parts.append(input_part.astype(jnp.bfloat16))
        gate_parts.append(gate_part.astype(jnp.bfloat16))
        owner_gu.append(weight_gu)
        owner_down.append(weight_down)
    helper_gu = owner_gu[owned_experts].astype(jnp.bfloat16)
    helper_down = owner_down[owned_experts].astype(jnp.bfloat16)
    back_gu, back_down = (
        lax.all_to_all(
            helper_gu.reshape(2, devices, piece_rows, features),
            "expert",
            split_axis=1,
            concat_axis=1,
            tiled=True,
        ),
        lax.all_to_all(
            helper_down.reshape(1, devices, piece_rows, features),
            "expert",
            split_axis=1,
            concat_axis=1,
            tiled=True,
        ),
    )
    back_gu = jnp.take(back_gu, helper_of_owner, axis=1)
    back_down = jnp.take(back_down, helper_of_owner, axis=1)
    extra_gu, extra_down = (
        lax.all_to_all(back_gu, "expert", split_axis=1, concat_axis=1, tiled=True),
        lax.all_to_all(back_down, "expert", split_axis=1, concat_axis=1, tiled=True),
    )
    extra_gu = extra_gu.reshape(2, quarter, features).astype(jnp.float32)
    extra_down = extra_down.reshape(quarter, features).astype(jnp.float32)
    stacked_dx = jnp.stack(input_parts, axis=0)
    stacked_dg = jnp.stack(gate_parts, axis=0)
    summed_dx, summed_dg = (
        lax.psum_scatter(stacked_dx, "dp", scatter_dimension=1, tiled=True).astype(jnp.float32),
        lax.psum_scatter(stacked_dg, "dp", scatter_dimension=1, tiled=True).astype(jnp.float32),
    )
    row_dx = summed_dx.astype(jnp.bfloat16)
    row_dg = summed_dg.astype(jnp.bfloat16)
    home_dx, home_dg = (
        lax.all_to_all(row_dx, "expert", split_axis=1, concat_axis=1, tiled=True),
        lax.all_to_all(row_dg, "expert", split_axis=1, concat_axis=1, tiled=True),
    )
    home_dx = home_dx.reshape(blocks * lane_rows, features)
    home_dg = home_dg.reshape(blocks * lane_rows).astype(jnp.float32)
    grad_tokens = jnp.einsum(
        "st,sd->td", home_picker, home_dx, preferred_element_type=jnp.float32
    ).astype(jnp.bfloat16)
    grad_gates = jnp.sum(jnp.where(home_matches, home_dg[:, None, None], 0.0), axis=0)
    grad_gu = []
    grad_down = []
    for block in range(owned_experts):
        present = (copied_local == block).astype(jnp.float32)
        grad_gu.append((owner_gu[block] + present * extra_gu).astype(jnp.bfloat16))
        grad_down.append((owner_down[block] + present * extra_down).astype(jnp.bfloat16))
    return (grad_tokens, grad_gates, jnp.stack(grad_gu, axis=0), jnp.stack(grad_down, axis=0))


def solution(mesh):
    in_specs = (
        P(("dp", "expert"), None),
        P(("dp", "expert"), None),
        P(("dp", "expert"), None),
        P(("dp", "expert"), None),
        P(("dp", "expert"), None),
        P(),
        P("expert", None, "dp", None),
        P("expert", "dp", None),
    )
    out_specs = (
        P(("dp", "expert"), None),
        P(("dp", "expert"), None),
        P("expert", None, "dp", None),
        P("expert", "dp", None),
    )
    return jax.shard_map(shards, mesh=mesh, in_specs=in_specs, out_specs=out_specs, check_vma=False)
```

profile of v0, /device:TPU:0, one launch (start us, length us, event | category | flops | bytes accessed | tf_op | source)
XLA Modules:
  0.0 546.3 jit_solution(6755420541427667318)
XLA Ops:
  11.6 1.4 copy.113
  13.0 55.2 %all_to_all.73 = bf16[3,128,2048]{2,0,1:T(4,128)(2,1)S(1)} all-to-all(bf16[3,128,2048]{2,0,1:T(4,128)(2,1)S(1)} %copy.113), channel_id=1, replica_groups=mesh['dp'=4,'expert'=8] {'expert'}, dimensions={1} | all-to-all | bytes 3145728 | tf_op jit(solution)/shard_map/all_to_all | solution.py:93
  68.2 2.3 copy.114
  71.1 1.4 copy.111
  72.5 51.5 %all_to_all.74 = bf16[3,128,2048]{2,0,1:T(4,128)(2,1)S(1)} all-to-all(bf16[3,128,2048]{2,0,1:T(4,128)(2,1)S(1)} %copy.111), channel_id=1, replica_groups=mesh['dp'=4,'expert'=8] {'expert'}, dimensions={1} | all-to-all | bytes 3145728 | tf_op jit(solution)/shard_map/all_to_all | solution.py:100
  124.0 2.3 copy.112
  129.1 1.3 copy.116
  130.4 3.7 all-to-all-start.5
  135.1 36.7 %all-to-all-done.5 = bf16[2,8,24,2048]{3,2,0,1:T(8,128)(2,1)S(1)} async-done(((bf16[2,8,24,2048]{3,2,0,1:T(8,128)(2,1)}), bf16[2,8,24,2048]{3,2,0,1:T(8,128)(2,1)S(1)}, u32[]{:S(2)}, u32[]{:S(2)}) %all-to-all-start.5) | async-done | bytes 1572896 | tf_op jit(solution)/shard_map/all_to_all | solution.py:127
  171.8 4.2 all-to-all-start.3
  176.9 1.4 select_bitcast_fusion.1
  178.2 18.7 %all-to-all-done.3 = bf16[1,8,24,2048]{3,2,0,1:T(8,128)(2,1)} async-done(((bf16[1,8,24,2048]{3,2,0,1:T(8,128)(2,1)}), bf16[1,8,24,2048]{3,2,0,1:T(8,128)(2,1)}, u32[]{:S(2)}, u32[]{:S(2)}) %all-to-all-start.3) | async-done | bytes 786464 | tf_op jit(solution)/shard_map/all_to_all | solution.py:134
  197.0 3.6 all-to-all-start.6
  200.6 1.7 gather_fusion
  202.3 1.0 fusion.42
  203.4 34.9 %all-to-all-done.6 = bf16[2,8,24,2048]{3,2,0,1:T(8,128)(2,1)S(1)} async-done(((bf16[2,8,24,2048]{3,2,0,1:T(8,128)(2,1)}), bf16[2,8,24,2048]{3,2,0,1:T(8,128)(2,1)S(1)}, u32[]{:S(2)}, u32[]{:S(2)}) %all-to-all-start.6) | async-done | bytes 1572896 | tf_op jit(solution)/shard_map/all_to_all | solution.py:145
  238.3 4.2 all-to-all-start.4
  242.9 2.6 fusion.34
  245.7 17.8 %all-to-all-done.4 = bf16[1,8,24,2048]{3,2,0,1:T(8,128)(2,1)} async-done(((bf16[1,8,24,2048]{3,2,0,1:T(8,128)(2,1)}), bf16[1,8,24,2048]{3,2,0,1:T(8,128)(2,1)}, u32[]{:S(2)}, u32[]{:S(2)}) %all-to-all-start.4) | async-done | bytes 786464 | tf_op jit(solution)/shard_map/all_to_all | solution.py:146
  263.5 2.8 fusion.8
  266.3 3.2 fusion.35
  270.6 1.1 copy-done.5
  271.7 2.6 fusion.38
  275.9 1.5 copy.130
  277.4 23.2 %reduce-scatter.7.cloned.1.call-done = bf16[128,3]{1,0:T(8,128)(2,1)} async-done(((bf16[512,3]{1,0:T(8,128)(2,1)}), bf16[128,3]{1,0:T(8,128)(2,1)}) %reduce-scatter.7.cloned.1.call-update) | async-done | bytes 784
  300.7 1.5 copy.121
  302.1 4.6 all-to-all-start.8
  306.8 1.4 copy.108
  308.1 4.0 all-to-all-done.8
  312.1 1.3 copy_convert_fusion
  313.4 1.4 reshape.297
  314.8 1.5 select_reduce_fusion
  317.0 8.0 %all_to_all.75 = bf16[3,8,16]{2,0,1:T(4,128)(2,1)S(1)} all-to-all(bf16[3,8,16]{2,0,1:T(4,128)(2,1)S(1)} %copy.109), channel_id=1, replica_groups=mesh['dp'=4,'expert'=8] {'expert'}, dimensions={1} | all-to-all | bytes 1536 | tf_op jit(solution)/shard_map/all_to_all | solution.py:107
  325.1 8.2 %all_gather.9 = bf16[3,512]{1,0:T(4,128)(2,1)S(1)} all-gather(bf16[3,128]{1,0:T(4,128)(2,1)S(1)} %all_to_all.46), channel_id=1, replica_groups=mesh['dp'=4,'expert'=8] {'dp'}, dimensions={1}, use_global_device_ids=true | all-gather | bytes 3840 | tf_op jit(solution)/shard_map/all_gather | solution.py:114
  333.4 2.9 fusion.99
  336.4 1.3 fusion.13
  338.7 1.0 fusion.98
  340.6 1.3 fusion.12
  341.9 1.0 fusion.97
  343.0 1.3 fusion.11
  344.3 3.2 pad_maximum_fusion
  348.5 3.2 convolution_convert_fusion.3
  351.7 3.5 all-to-all-start.11
  355.3 2.6 convolution_convert_fusion.2
  357.8 1.2 copy.123
  359.1 17.0 %all-to-all-done.11 = bf16[1,8,24,2048]{3,2,0,1:T(8,128)(2,1)S(1)} async-done(((bf16[1,8,24,2048]{3,2,0,1:T(8,128)(2,1)}), bf16[1,8,24,2048]{3,2,0,1:T(8,128)(2,1)S(1)}, u32[]{:S(2)}, u32[]{:S(2)}) %all-to-all-start.11) | async-done | bytes 786464 | tf_op jit(solution)/shard_map/all_to_all | solution.py:178
  376.1 3.6 all-to-all-start.9
  381.5 35.9 %all-to-all-done.9 = bf16[2,8,24,2048]{3,2,0,1:T(8,128)(2,1)S(1)} async-done(((bf16[2,8,24,2048]{3,2,0,1:T(8,128)(2,1)}), bf16[2,8,24,2048]{3,2,0,1:T(8,128)(2,1)S(1)}, u32[]{:S(2)}, u32[]{:S(2)}) %all-to-all-start.9) | async-done | bytes 1572896 | tf_op jit(solution)/shard_map/all_to_all | solution.py:171
  417.4 4.2 all-to-all-start.12
  422.5 1.4 select_bitcast_fusion
  423.8 18.8 %all-to-all-done.12 = bf16[1,8,24,2048]{3,2,0,1:T(8,128)(2,1)} async-done(((bf16[1,8,24,2048]{3,2,0,1:T(8,128)(2,1)}), bf16[1,8,24,2048]{3,2,0,1:T(8,128)(2,1)}, u32[]{:S(2)}, u32[]{:S(2)}) %all-to-all-start.12) | async-done | bytes 786464 | tf_op jit(solution)/shard_map/all_to_all | solution.py:190
  442.6 3.6 all-to-all-start.10
  448.1 4.1 copy.119
  452.2 31.7 %all-to-all-done.10 = bf16[2,8,24,2048]{3,2,0,1:T(8,128)(2,1)S(1)} async-done(((bf16[2,8,24,2048]{3,2,0,1:T(8,128)(2,1)}), bf16[2,8,24,2048]{3,2,0,1:T(8,128)(2,1)S(1)}, u32[]{:S(2)}, u32[]{:S(2)}) %all-to-all-start.10) | async-done | bytes 1572896 | tf_op jit(solution)/shard_map/all_to_all | solution.py:189
  483.9 1.1 copy-done.2
  485.0 3.9 all-to-all-start.7
  488.9 1.5 convert_multiply_fusion.6
  490.4 2.3 fusion.18
  492.8 2.3 fusion.19
  495.1 1.3 pad_maximum_fusion.2
  502.2 1.9 pad_maximum_fusion.1
  504.2 33.4 %all-to-all-done.7 = bf16[3,128,2048]{2,0,1:T(4,128)(2,1)S(1)} async-done(((bf16[3,128,2048]{2,0,1:T(4,128)(2,1)}), bf16[3,128,2048]{2,0,1:T(4,128)(2,1)S(1)}, u32[]{:S(2)}, u32[]{:S(2)}) %all-to-all-start.7) | async-done | bytes 1572896 | tf_op jit(solution)/shard_map/all_to_all | solution.py:203
  537.6 1.1 copy.120
  538.8 1.0 convolution_convert_fusion.4
  (139 shorter events, 23.5 us)
Async XLA Ops:
  7.2 3.9 copy-start
  7.2 235.8 %all-gather.5.cloned.1.call-start = ((), (), s32[]{:S(2)}) async-start(), calls=%async_computation.16 | async-start | bytes 7864320 | tf_op jit(solution)/shard_map/all_gather | solution.py:112
  11.0 59.5 %copy-start.12 = (bf16[384,32]{0,1:T(8,128)(2,1)}, bf16[384,32]{0,1:T(8,128)(2,1)S(1)}, u32[]{:S(2)}) copy-start(bf16[384,32]{0,1:T(8,128)(2,1)S(1)} %convert_reduce_fusion) | copy-start | bytes 73732
  68.2 2.4 copy-start.24
  70.5 193.0 %all-gather.3.cloned.1.call-start = ((), (), s32[]{:S(2)}) async-start(), calls=%async_computation.15 | async-start | bytes 7864320 | tf_op jit(solution)/shard_map/all_gather | solution.py:113
  124.0 2.3 copy-start.26
  124.0 4.9 copy-start.4
  126.3 4.0 copy-start.27
  130.4 3.7 copy-start.9
  130.4 41.4 %all-to-all-start.5 = ((bf16[2,8,24,2048]{3,2,0,1:T(8,128)(2,1)}), bf16[2,8,24,2048]{3,2,0,1:T(8,128)(2,1)S(1)}, u32[]{:S(2)}, u32[]{:S(2)}) async-start(bf16[2,8,24,2048]{3,2,0,1:T(8,128)(2,1)} %copy.116), calls=%async_computation.5 | async-start | bytes 3145728 | tf_op jit(solution)/shard_map/all_to_all | solution.py:127
  171.8 25.2 %all-to-all-start.3 = ((bf16[1,8,24,2048]{3,2,0,1:T(8,128)(2,1)}), bf16[1,8,24,2048]{3,2,0,1:T(8,128)(2,1)}, u32[]{:S(2)}, u32[]{:S(2)}) async-start(bf16[1,8,24,2048]{3,2,0,1:T(8,128)(2,1)} %bitcast.30), calls=%async_computation.3 | async-start | bytes 1572864 | tf_op jit(solution)/shard_map/all_to_all | solution.py:134
  197.0 41.3 %all-to-all-start.6 = ((bf16[2,8,24,2048]{3,2,0,1:T(8,128)(2,1)}), bf16[2,8,24,2048]{3,2,0,1:T(8,128)(2,1)S(1)}, u32[]{:S(2)}, u32[]{:S(2)}) async-start(bf16[2,8,24,2048]{3,2,0,1:T(8,128)(2,1)} %select_bitcast_fusion.1), calls=%async_computation.6 | async-start | bytes 3145728 | tf_op jit(solution)/shard_map/all_to_all | solution.py:145
  238.3 25.2 %all-to-all-start.4 = ((bf16[1,8,24,2048]{3,2,0,1:T(8,128)(2,1)}), bf16[1,8,24,2048]{3,2,0,1:T(8,128)(2,1)}, u32[]{:S(2)}, u32[]{:S(2)}) async-start(bf16[1,8,24,2048]{3,2,0,1:T(8,128)(2,1)} %fusion.42), calls=%async_computation.4 | async-start | bytes 1572864 | tf_op jit(solution)/shard_map/all_to_all | solution.py:146
  242.5 58.2 %reduce-scatter.7.cloned.1.call-start = ((), (), s32[]{:S(2)}) async-start(), calls=%async_computation.18 | async-start | bytes 163840
  245.7 20.6 %copy-start.22 = (bf16[1,512,192]{1,2,0:T(8,128)(2,1)}, bf16[1,512,192]{1,2,0:T(8,128)(2,1)S(1)}, u32[]{:S(2)}) copy-start(bf16[1,512,192]{1,2,0:T(8,128)(2,1)S(1)} %multiply_convert_fusion) | copy-start | bytes 589828
  263.5 6.2 %slice-start.2 = ((s8[6291456]{0:T(1024)(128)(4,1)}), s8[4194304]{0:T(1024)(128)(4,1)S(1)}, s32[]{:S(2)}) async-start(s8[6291456]{0:T(1024)(128)(4,1)} %bitcast.321), calls=%async_computation.21 | async-start | bytes 8388608
  266.3 3.4 slice-start.3
  266.3 3.4 copy-start.10
  269.5 1.0 copy-start.7
  269.7 2.0 copy-start.5
  302.1 10.0 %all-to-all-start.8 = ((bf16[3,8,16]{2,0,1:T(4,128)(2,1)}), bf16[3,8,16]{2,0,1:T(4,128)(2,1)}, u32[]{:S(2)}, u32[]{:S(2)}) async-start(bf16[3,8,16]{2,0,1:T(4,128)(2,1)} %copy.121), calls=%async_computation.9 | async-start | bytes 16384 | tf_op jit(solution)/shard_map/all_to_all | solution.py:204
  306.7 141.4 %reduce-scatter.5.cloned.1.call-start = ((), (), s32[]{:S(2)}) async-start(), calls=%async_computation.17 | async-start | bytes 7864320 | tf_op jit(solution)/shard_map/reduce_scatter | solution.py:197
  333.4 4.3 slice-start.4
  336.3 1.4 copy-start.29
  336.3 1.4 copy-start.31
  336.3 1.8 slice-start.5
  336.3 1.9 copy-start.8
  336.4 2.4 copy-start.11
  338.7 1.9 copy-start.6
  339.8 2.1 copy-start.14
  339.8 2.1 copy-start.16
  343.0 1.3 copy-start.18
  343.0 1.3 copy-start.20
  347.5 0.9 copy-start.23
  348.5 6.8 %copy-start.30 = (bf16[1,512,192]{1,2,0:T(8,128)(2,1)S(1)}, bf16[1,512,192]{1,2,0:T(8,128)(2,1)}, u32[]{:S(2)}) copy-start(bf16[1,512,192]{1,2,0:T(8,128)(2,1)} %copy-done.29) | copy-start | bytes 589828
  348.5 6.8 %copy-start.32 = (bf16[1,512,192]{1,2,0:T(8,128)(2,1)S(1)}, bf16[1,512,192]{1,2,0:T(8,128)(2,1)}, u32[]{:S(2)}) copy-start(bf16[1,512,192]{1,2,0:T(8,128)(2,1)} %copy-done.31) | copy-start | bytes 589828
  351.7 24.4 %all-to-all-start.11 = ((bf16[1,8,24,2048]{3,2,0,1:T(8,128)(2,1)}), bf16[1,8,24,2048]{3,2,0,1:T(8,128)(2,1)S(1)}, u32[]{:S(2)}, u32[]{:S(2)}) async-start(bf16[1,8,24,2048]{3,2,0,1:T(8,128)(2,1)} %bitcast.61), calls=%async_computation.12 | async-start | bytes 1572864 | tf_op jit(solution)/shard_map/all_to_all | solution.py:178
  359.1 20.6 %copy-start.28 = (s32[8]{0:T(128)S(1)}, s32[8]{0:T(128)}, u32[]{:S(2)}) copy-start(s32[8]{0:T(128)} %copy-done.27) | copy-start | bytes 100
  376.1 41.3 %all-to-all-start.9 = ((bf16[2,8,24,2048]{3,2,0,1:T(8,128)(2,1)}), bf16[2,8,24,2048]{3,2,0,1:T(8,128)(2,1)S(1)}, u32[]{:S(2)}, u32[]{:S(2)}) async-start(bf16[2,8,24,2048]{3,2,0,1:T(8,128)(2,1)} %copy.123), calls=%async_computation.10 | async-start | bytes 3145728 | tf_op jit(solution)/shard_map/all_to_all | solution.py:171
  417.4 25.2 %all-to-all-start.12 = ((bf16[1,8,24,2048]{3,2,0,1:T(8,128)(2,1)}), bf16[1,8,24,2048]{3,2,0,1:T(8,128)(2,1)}, u32[]{:S(2)}, u32[]{:S(2)}) async-start(bf16[1,8,24,2048]{3,2,0,1:T(8,128)(2,1)} %fusion.41), calls=%async_computation.13 | async-start | bytes 1572864 | tf_op jit(solution)/shard_map/all_to_all | solution.py:190
  423.8 23.6 %copy-start.25 = (f32[32,8]{1,0:T(8,128)S(1)}, f32[32,8]{1,0:T(8,128)}, u32[]{:S(2)}) copy-start(f32[32,8]{1,0:T(8,128)} %get-tuple-element.14) | copy-start | bytes 3076
  442.6 41.3 %all-to-all-start.10 = ((bf16[2,8,24,2048]{3,2,0,1:T(8,128)(2,1)}), bf16[2,8,24,2048]{3,2,0,1:T(8,128)(2,1)S(1)}, u32[]{:S(2)}, u32[]{:S(2)}) async-start(bf16[2,8,24,2048]{3,2,0,1:T(8,128)(2,1)} %select_bitcast_fusion), calls=%async_computation.11 | async-start | bytes 3145728 | tf_op jit(solution)/shard_map/all_to_all | solution.py:189
  483.9 1.1 copy-start.2
  485.0 52.6 %all-to-all-start.7 = ((bf16[3,128,2048]{2,0,1:T(4,128)(2,1)}), bf16[3,128,2048]{2,0,1:T(4,128)(2,1)S(1)}, u32[]{:S(2)}, u32[]{:S(2)}) async-start(bf16[3,128,2048]{2,0,1:T(4,128)(2,1)} %copy.119), calls=%async_computation.8 | async-start | bytes 4194304 | tf_op jit(solution)/shard_map/all_to_all | solution.py:203
  495.1 2.0 copy-start.3
  497.1 2.2 slice-start
  497.9 2.3 slice-start.1
  498.3 1.9 copy-start.15
  498.3 1.9 copy-start.17
  500.2 1.0 copy-start.19
  500.2 1.0 copy-start.21
  502.2 37.6 %copy-start.1 = (bf16[32,2048]{1,0:T(8,128)(2,1)S(1)}, bf16[32,2048]{1,0:T(8,128)(2,1)}, u32[]{:S(2)}) copy-start(bf16[32,2048]{1,0:T(8,128)(2,1)} %param.12) | copy-start | bytes 393220
  504.2 34.6 %copy-start.13 = (bf16[384,32]{0,1:T(8,128)(2,1)S(1)}, bf16[384,32]{0,1:T(8,128)(2,1)}, u32[]{:S(2)}) copy-start(bf16[384,32]{0,1:T(8,128)(2,1)} %copy-done.12) | copy-start | bytes 73732
Sparse Core Ops, SparseCore 0:
  70.6 68.9 all-gather.4
  141.4 70.0 all-gather.2
  277.6 23.0 reduce-scatter.6
  347.7 67.2 reduce-scatter.4
where the time goes:
time: 548 us; the launch traced here: 546 us
  waiting for transfers between devices  272 us (50%)
  blocking collectives  123 us (22%)
  starting transfers between devices  39.4 us (7%)
  matrix products  36.4 us (7%)
  local copies, waits for them, and re-layouts  35.9 us (7%)
  other arithmetic  21.5 us (4%)
  between operations  17.8 us (3%)
    all_to_all x1, blocking collectives, shards(): lax.all_to_all(row_x.reshape(blocks, lane_rows, features), 'expert', spli...  55.2 us
    all_to_all x1, blocking collectives, shards(): lax.all_to_all(row_dy.reshape(blocks, lane_rows, features), 'expert', spl...  51.5 us
    all_to_all x1, waiting for transfers between devices, shards(): lax.all_to_all(source_gu.reshape(2, devices, piece_rows, features), 'expe...  36.7 us
    all_to_all x1, waiting for transfers between devices, shards(): lax.all_to_all(helper_gu.reshape(2, devices, piece_rows, features), 'expe...  35.9 us
    all_to_all x1, waiting for transfers between devices, shards(): lax.all_to_all(spread_gu, 'expert', split_axis=1, concat_axis=1, tiled=True)  34.9 us
    all_to_all x1, waiting for transfers between devices, shards(): lax.all_to_all(row_dx, 'expert', split_axis=1, concat_axis=1, tiled=True)  33.4 us
    all_to_all x1, waiting for transfers between devices, shards(): lax.all_to_all(back_gu, 'expert', split_axis=1, concat_axis=1, tiled=True)  31.7 us
    unnamed x5, waiting for transfers between devices  23.3 us
  transfers between devices with their start and end apart: 14, of which 11 were waited for; matrix products, arithmetic and copies ran while one was open for 8% of the time, Pallas kernels for 0%

commit v1 on v0

--- a/solution.py
+++ b/solution.py
@@ -2,6 +2,13 @@
 import jax.numpy as jnp
 from jax import lax
 from jax.sharding import PartitionSpec as P
+
+search_frame_in = lambda z_in, pos_dim, at_axis: jnp.concatenate(
+    jax.lax.all_to_all(
+        jnp.stack(jnp.split(z_in, jax.lax.axis_size("expert"), pos_dim), axis=0), "expert", 0, 0
+    ),
+    at_axis,
+)
 
 
 def lookup(values_table, indices):
@@ -200,7 +207,7 @@
     row_dx = summed_dx.astype(jnp.bfloat16)
     row_dg = summed_dg.astype(jnp.bfloat16)
     home_dx, home_dg = (
-        lax.all_to_all(row_dx, "expert", split_axis=1, concat_axis=1, tiled=True),
+        search_frame_in(row_dx, 1, 1),
         lax.all_to_all(row_dg, "expert", split_axis=1, concat_axis=1, tiled=True),
     )
     home_dx = home_dx.reshape(blocks * lane_rows, features)

time: 548 us -> 530 us (0.967)
  waiting for transfers between devices: 272 us -> 259 us
    all_to_all x1, waiting for transfers between devices: 33.4 us -> 22.8 us  [jax.lax.all_to_all(jnp.stack(jnp.split(z_in, jax.lax.axis_size('expert'),...]
    unnamed x80 -> x81, local copies, waits for them, and re-layouts: 9.58 us -> 15.7 us
  transfers between devices with their start and end apart: 14 -> 14, of which waited for: 11 -> 11; matrix products, arithmetic and copies ran while one was open for 8% -> 9% of each run, Pallas kernels for 0% -> 0%
where the time goes in v1:
time: 530 us; the launch traced here: 528 us
  waiting for transfers between devices  259 us (49%)
  blocking collectives  123 us (23%)
  starting transfers between devices  39.5 us (7%)
  matrix products  36.5 us (7%)
  local copies, waits for them, and re-layouts  34.7 us (7%)
  other arithmetic  18.4 us (3%)
  between operations  17.8 us (3%)
    all_to_all x1, blocking collectives, shards(): lax.all_to_all(row_x.reshape(blocks, lane_rows, features), 'expert', spli...  55.2 us
    all_to_all x1, blocking collectives, shards(): lax.all_to_all(row_dy.reshape(blocks, lane_rows, features), 'expert', spl...  51.5 us
    all_to_all x1, waiting for transfers between devices, shards(): lax.all_to_all(source_gu.reshape(2, devices, piece_rows, features), 'expe...  36.8 us
    all_to_all x1, waiting for transfers between devices, shards(): lax.all_to_all(helper_gu.reshape(2, devices, piece_rows, features), 'expe...  35.9 us
    all_to_all x1, waiting for transfers between devices, shards(): lax.all_to_all(spread_gu, 'expert', split_axis=1, concat_axis=1, tiled=True)  35 us
    all_to_all x1, waiting for transfers between devices, shards(): lax.all_to_all(back_gu, 'expert', split_axis=1, concat_axis=1, tiled=True)  29.9 us
    unnamed x5, waiting for transfers between devices  23.3 us
    all_to_all x1, waiting for transfers between devices, jax.lax.all_to_all(jnp.stack(jnp.split(z_in, jax.lax.axis_size('expert'),...  22.8 us
  transfers between devices with their start and end apart: 14, of which 11 were waited for; matrix products, arithmetic and copies ran while one was open for 9% of the time, Pallas kernels for 0%

profile of v1, /device:TPU:0, one launch (start us, length us, event | category | flops | bytes accessed | tf_op | source)
XLA Modules:
  0.0 528.3 jit_solution(6579140861374855946)
XLA Ops:
  11.6 1.4 copy.112
  13.0 55.2 %all_to_all.73 = bf16[3,128,2048]{2,0,1:T(4,128)(2,1)S(1)} all-to-all(bf16[3,128,2048]{2,0,1:T(4,128)(2,1)S(1)} %copy.112), channel_id=1, replica_groups=mesh['dp'=4,'expert'=8] {'expert'}, dimensions={1} | all-to-all | bytes 3145728 | tf_op jit(solution)/shard_map/all_to_all | solution.py:100
  68.2 2.3 copy.113
  71.1 1.4 copy.110
  72.5 51.5 %all_to_all.74 = bf16[3,128,2048]{2,0,1:T(4,128)(2,1)S(1)} all-to-all(bf16[3,128,2048]{2,0,1:T(4,128)(2,1)S(1)} %copy.110), channel_id=1, replica_groups=mesh['dp'=4,'expert'=8] {'expert'}, dimensions={1} | all-to-all | bytes 3145728 | tf_op jit(solution)/shard_map/all_to_all | solution.py:107
  124.0 2.3 copy.111
  129.1 1.3 copy.115
  130.3 3.7 all-to-all-start.5
  134.1 0.9 constant_dynamic-slice_fusion.1
  135.0 36.8 %all-to-all-done.5 = bf16[2,8,24,2048]{3,2,0,1:T(8,128)(2,1)S(1)} async-done(((bf16[2,8,24,2048]{3,2,0,1:T(8,128)(2,1)}), bf16[2,8,24,2048]{3,2,0,1:T(8,128)(2,1)S(1)}, u32[]{:S(2)}, u32[]{:S(2)}) %all-to-all-start.5) | async-done | bytes 1572896 | tf_op jit(solution)/shard_map/all_to_all | solution.py:134
  171.8 4.2 all-to-all-start.3
  176.8 1.4 select_bitcast_fusion.1
  178.2 18.7 %all-to-all-done.3 = bf16[1,8,24,2048]{3,2,0,1:T(8,128)(2,1)} async-done(((bf16[1,8,24,2048]{3,2,0,1:T(8,128)(2,1)}), bf16[1,8,24,2048]{3,2,0,1:T(8,128)(2,1)}, u32[]{:S(2)}, u32[]{:S(2)}) %all-to-all-start.3) | async-done | bytes 786464 | tf_op jit(solution)/shard_map/all_to_all | solution.py:141
  196.9 3.6 all-to-all-start.6
  200.5 1.7 gather_fusion
  202.3 1.0 fusion.42
  203.3 35.0 %all-to-all-done.6 = bf16[2,8,24,2048]{3,2,0,1:T(8,128)(2,1)S(1)} async-done(((bf16[2,8,24,2048]{3,2,0,1:T(8,128)(2,1)}), bf16[2,8,24,2048]{3,2,0,1:T(8,128)(2,1)S(1)}, u32[]{:S(2)}, u32[]{:S(2)}) %all-to-all-start.6) | async-done | bytes 1572896 | tf_op jit(solution)/shard_map/all_to_all | solution.py:152
  238.3 4.2 all-to-all-start.4
  242.9 2.6 fusion.34
  245.7 17.8 %all-to-all-done.4 = bf16[1,8,24,2048]{3,2,0,1:T(8,128)(2,1)} async-done(((bf16[1,8,24,2048]{3,2,0,1:T(8,128)(2,1)}), bf16[1,8,24,2048]{3,2,0,1:T(8,128)(2,1)}, u32[]{:S(2)}, u32[]{:S(2)}) %all-to-all-start.4) | async-done | bytes 786464 | tf_op jit(solution)/shard_map/all_to_all | solution.py:153
  263.4 2.8 fusion.8
  266.3 3.2 fusion.35
  271.4 1.1 copy-done.6
  272.5 2.6 fusion.38
  277.0 23.2 %reduce-scatter.7.cloned.1.call-done = bf16[128,3]{1,0:T(8,128)(2,1)} async-done(((bf16[512,3]{1,0:T(8,128)(2,1)}), bf16[128,3]{1,0:T(8,128)(2,1)}) %reduce-scatter.7.cloned.1.call-update) | async-done | bytes 784
  300.2 1.5 copy.119
  301.7 4.6 all-to-all-start.8
  306.4 5.5 %all-to-all-done.8 = bf16[3,8,16]{2,0,1:T(4,128)(2,1)S(1)} async-done(((bf16[3,8,16]{2,0,1:T(4,128)(2,1)}), bf16[3,8,16]{2,0,1:T(4,128)(2,1)S(1)}, u32[]{:S(2)}, u32[]{:S(2)}) %all-to-all-start.8) | async-done | bytes 800 | tf_op jit(solution)/shard_map/all_to_all | solution.py:211
  312.3 8.0 %all_to_all.75 = bf16[3,8,16]{2,0,1:T(4,128)(2,1)S(1)} all-to-all(bf16[3,8,16]{2,0,1:T(4,128)(2,1)S(1)} %copy.108), channel_id=1, replica_groups=mesh['dp'=4,'expert'=8] {'expert'}, dimensions={1} | all-to-all | bytes 1536 | tf_op jit(solution)/shard_map/all_to_all | solution.py:114
  320.4 8.2 %all_gather.9 = bf16[3,512]{1,0:T(4,128)(2,1)S(1)} all-gather(bf16[3,128]{1,0:T(4,128)(2,1)S(1)} %all_to_all.46), channel_id=1, replica_groups=mesh['dp'=4,'expert'=8] {'dp'}, dimensions={1}, use_global_device_ids=true | all-gather | bytes 3840 | tf_op jit(solution)/shard_map/all_gather | solution.py:121
  328.6 2.9 fusion.107
  331.6 1.3 fusion.13
  334.0 1.0 fusion.106
  335.9 1.3 fusion.12
  337.2 1.0 fusion.105
  338.2 1.3 fusion.11
  339.5 3.3 pad_maximum_fusion
  343.7 3.2 convolution_convert_fusion.3
  347.0 3.5 all-to-all-start.11
  350.6 2.6 convolution_convert_fusion.2
  353.1 1.2 copy.121
  354.4 17.0 %all-to-all-done.11 = bf16[1,8,24,2048]{3,2,0,1:T(8,128)(2,1)S(1)} async-done(((bf16[1,8,24,2048]{3,2,0,1:T(8,128)(2,1)}), bf16[1,8,24,2048]{3,2,0,1:T(8,128)(2,1)S(1)}, u32[]{:S(2)}, u32[]{:S(2)}) %all-to-all-start.11) | async-done | bytes 786464 | tf_op jit(solution)/shard_map/all_to_all | solution.py:185
  371.4 3.6 all-to-all-start.9
  375.7 1.0 fusion.41
  376.8 35.9 %all-to-all-done.9 = bf16[2,8,24,2048]{3,2,0,1:T(8,128)(2,1)S(1)} async-done(((bf16[2,8,24,2048]{3,2,0,1:T(8,128)(2,1)}), bf16[2,8,24,2048]{3,2,0,1:T(8,128)(2,1)S(1)}, u32[]{:S(2)}, u32[]{:S(2)}) %all-to-all-start.9) | async-done | bytes 1572896 | tf_op jit(solution)/shard_map/all_to_all | solution.py:178
  412.7 4.2 all-to-all-start.12
  419.7 1.4 select_bitcast_fusion
  422.0 15.9 %all-to-all-done.12 = bf16[1,8,24,2048]{3,2,0,1:T(8,128)(2,1)} async-done(((bf16[1,8,24,2048]{3,2,0,1:T(8,128)(2,1)}), bf16[1,8,24,2048]{3,2,0,1:T(8,128)(2,1)}, u32[]{:S(2)}, u32[]{:S(2)}) %all-to-all-start.12) | async-done | bytes 786464 | tf_op jit(solution)/shard_map/all_to_all | solution.py:197
  437.9 3.6 all-to-all-start.10
  441.5 0.9 fusion.94
  442.4 0.9 fusion.93
  444.3 0.9 fusion.91
  448.1 1.1 copy-done.2
  449.3 29.9 %all-to-all-done.10 = bf16[2,8,24,2048]{3,2,0,1:T(8,128)(2,1)S(1)} async-done(((bf16[2,8,24,2048]{3,2,0,1:T(8,128)(2,1)}), bf16[2,8,24,2048]{3,2,0,1:T(8,128)(2,1)S(1)}, u32[]{:S(2)}, u32[]{:S(2)}) %all-to-all-start.10) | async-done | bytes 1572896 | tf_op jit(solution)/shard_map/all_to_all | solution.py:196
  479.2 3.8 all-to-all-start.7
  483.1 1.5 convert_multiply_fusion.6
  484.6 2.4 fusion.18
  487.0 2.3 fusion.19
  489.3 1.3 pad_maximum_fusion.2
  493.7 1.0 fusion.15
  494.7 1.0 fusion.14
  495.7 1.9 pad_maximum_fusion.1
  497.7 22.8 %all-to-all-done.7 = bf16[8,3,16,2048]{3,2,1,0:T(8,128)(2,1)S(1)} async-done(((bf16[8,3,16,2048]{3,2,1,0:T(8,128)(2,1)}), bf16[8,3,16,2048]{3,2,1,0:T(8,128)(2,1)S(1)}, u32[]{:S(2)}, u32[]{:S(2)}) %all-to-all-start.7) | async-done | bytes 1572896 | tf_op jit(solution)/shard_map/all_to_all | solution.py:7
  520.7 1.1 convolution_convert_fusion.4
  (140 shorter events, 24.6 us)
Async XLA Ops:
  7.2 3.9 copy-start
  7.2 235.7 %all-gather.5.cloned.1.call-start = ((), (), s32[]{:S(2)}) async-start(), calls=%async_computation.16 | async-start | bytes 7864320 | tf_op jit(solution)/shard_map/all_gather | solution.py:119
  68.2 2.4 copy-start.23
  70.5 193.0 %all-gather.3.cloned.1.call-start = ((), (), s32[]{:S(2)}) async-start(), calls=%async_computation.15 | async-start | bytes 7864320 | tf_op jit(solution)/shard_map/all_gather | solution.py:120
  124.0 2.3 copy-start.25
  124.0 4.9 copy-start.5
  130.3 3.7 copy-start.10
  130.3 41.4 %all-to-all-start.5 = ((bf16[2,8,24,2048]{3,2,0,1:T(8,128)(2,1)}), bf16[2,8,24,2048]{3,2,0,1:T(8,128)(2,1)S(1)}, u32[]{:S(2)}, u32[]{:S(2)}) async-start(bf16[2,8,24,2048]{3,2,0,1:T(8,128)(2,1)} %copy.115), calls=%async_computation.5 | async-start | bytes 3145728 | tf_op jit(solution)/shard_map/all_to_all | solution.py:134
  171.8 25.2 %all-to-all-start.3 = ((bf16[1,8,24,2048]{3,2,0,1:T(8,128)(2,1)}), bf16[1,8,24,2048]{3,2,0,1:T(8,128)(2,1)}, u32[]{:S(2)}, u32[]{:S(2)}) async-start(bf16[1,8,24,2048]{3,2,0,1:T(8,128)(2,1)} %bitcast.30), calls=%async_computation.3 | async-start | bytes 1572864 | tf_op jit(solution)/shard_map/all_to_all | solution.py:141
  196.9 41.3 %all-to-all-start.6 = ((bf16[2,8,24,2048]{3,2,0,1:T(8,128)(2,1)}), bf16[2,8,24,2048]{3,2,0,1:T(8,128)(2,1)S(1)}, u32[]{:S(2)}, u32[]{:S(2)}) async-start(bf16[2,8,24,2048]{3,2,0,1:T(8,128)(2,1)} %select_bitcast_fusion.1), calls=%async_computation.6 | async-start | bytes 3145728 | tf_op jit(solution)/shard_map/all_to_all | solution.py:152
  238.3 25.2 %all-to-all-start.4 = ((bf16[1,8,24,2048]{3,2,0,1:T(8,128)(2,1)}), bf16[1,8,24,2048]{3,2,0,1:T(8,128)(2,1)}, u32[]{:S(2)}, u32[]{:S(2)}) async-start(bf16[1,8,24,2048]{3,2,0,1:T(8,128)(2,1)} %fusion.42), calls=%async_computation.4 | async-start | bytes 1572864 | tf_op jit(solution)/shard_map/all_to_all | solution.py:153
  242.5 57.7 %reduce-scatter.7.cloned.1.call-start = ((), (), s32[]{:S(2)}) async-start(), calls=%async_computation.18 | async-start | bytes 163840
  245.7 20.6 %copy-start.21 = (bf16[1,512,192]{1,2,0:T(8,128)(2,1)}, bf16[1,512,192]{1,2,0:T(8,128)(2,1)S(1)}, u32[]{:S(2)}) copy-start(bf16[1,512,192]{1,2,0:T(8,128)(2,1)S(1)} %multiply_convert_fusion) | copy-start | bytes 589828
  263.4 7.1 %slice-start.2 = ((s8[6291456]{0:T(1024)(128)(4,1)}), s8[4194304]{0:T(1024)(128)(4,1)S(1)}, s32[]{:S(2)}) async-start(s8[6291456]{0:T(1024)(128)(4,1)} %bitcast.355), calls=%async_computation.21 | async-start | bytes 8388608
  266.3 4.2 slice-start.3
  266.3 4.2 copy-start.11
  269.5 0.9 copy-start.8
  270.5 0.9 copy-start.3
  270.6 2.0 copy-start.6
  275.3 31.1 %copy-start.24 = (bf16[32,8]{0,1:T(8,128)(2,1)S(1)}, bf16[32,8]{0,1:T(8,128)(2,1)}, u32[]{:S(2)}) copy-start(bf16[32,8]{0,1:T(8,128)(2,1)} %param.16) | copy-start | bytes 1540
  301.7 10.2 %all-to-all-start.8 = ((bf16[3,8,16]{2,0,1:T(4,128)(2,1)}), bf16[3,8,16]{2,0,1:T(4,128)(2,1)S(1)}, u32[]{:S(2)}, u32[]{:S(2)}) async-start(bf16[3,8,16]{2,0,1:T(4,128)(2,1)} %copy.119), calls=%async_computation.9 | async-start | bytes 16384 | tf_op jit(solution)/shard_map/all_to_all | solution.py:211
  306.3 114.8 %reduce-scatter.5.cloned.1.call-start = ((), (), s32[]{:S(2)}) async-start(), calls=%async_computation.17 | async-start | bytes 7864320 | tf_op jit(solution)/shard_map/reduce_scatter | solution.py:204
  328.6 4.3 slice-start.4
  331.5 1.3 copy-start.26
  331.6 1.3 copy-start.28
  331.6 1.8 slice-start.5
  331.6 1.9 copy-start.9
  331.6 2.4 copy-start.12
  334.0 1.9 copy-start.7
  335.0 2.2 copy-start.13
  335.0 2.2 copy-start.15
  338.2 1.3 copy-start.17
  338.2 1.3 copy-start.19
  342.8 0.9 copy-start.22
  343.7 6.8 %copy-start.27 = (bf16[1,512,192]{1,2,0:T(8,128)(2,1)S(1)}, bf16[1,512,192]{1,2,0:T(8,128)(2,1)}, u32[]{:S(2)}) copy-start(bf16[1,512,192]{1,2,0:T(8,128)(2,1)} %copy-done.26) | copy-start | bytes 589828
  343.7 6.8 %copy-start.29 = (bf16[1,512,192]{1,2,0:T(8,128)(2,1)S(1)}, bf16[1,512,192]{1,2,0:T(8,128)(2,1)}, u32[]{:S(2)}) copy-start(bf16[1,512,192]{1,2,0:T(8,128)(2,1)} %copy-done.28) | copy-start | bytes 589828
  347.0 24.4 %all-to-all-start.11 = ((bf16[1,8,24,2048]{3,2,0,1:T(8,128)(2,1)}), bf16[1,8,24,2048]{3,2,0,1:T(8,128)(2,1)S(1)}, u32[]{:S(2)}, u32[]{:S(2)}) async-start(bf16[1,8,24,2048]{3,2,0,1:T(8,128)(2,1)} %bitcast.70), calls=%async_computation.12 | async-start | bytes 1572864 | tf_op jit(solution)/shard_map/all_to_all | solution.py:185
  371.4 41.3 %all-to-all-start.9 = ((bf16[2,8,24,2048]{3,2,0,1:T(8,128)(2,1)}), bf16[2,8,24,2048]{3,2,0,1:T(8,128)(2,1)S(1)}, u32[]{:S(2)}, u32[]{:S(2)}) async-start(bf16[2,8,24,2048]{3,2,0,1:T(8,128)(2,1)} %copy.121), calls=%async_computation.10 | async-start | bytes 3145728 | tf_op jit(solution)/shard_map/all_to_all | solution.py:178
  412.7 25.2 %all-to-all-start.12 = ((bf16[1,8,24,2048]{3,2,0,1:T(8,128)(2,1)}), bf16[1,8,24,2048]{3,2,0,1:T(8,128)(2,1)}, u32[]{:S(2)}, u32[]{:S(2)}) async-start(bf16[1,8,24,2048]{3,2,0,1:T(8,128)(2,1)} %fusion.41), calls=%async_computation.13 | async-start | bytes 1572864 | tf_op jit(solution)/shard_map/all_to_all | solution.py:197
  437.9 41.3 %all-to-all-start.10 = ((bf16[2,8,24,2048]{3,2,0,1:T(8,128)(2,1)}), bf16[2,8,24,2048]{3,2,0,1:T(8,128)(2,1)S(1)}, u32[]{:S(2)}, u32[]{:S(2)}) async-start(bf16[2,8,24,2048]{3,2,0,1:T(8,128)(2,1)} %select_bitcast_fusion), calls=%async_computation.11 | async-start | bytes 3145728 | tf_op jit(solution)/shard_map/all_to_all | solution.py:196
  448.1 1.1 copy-start.2
  479.2 41.3 %all-to-all-start.7 = ((bf16[8,3,16,2048]{3,2,1,0:T(8,128)(2,1)}), bf16[8,3,16,2048]{3,2,1,0:T(8,128)(2,1)S(1)}, u32[]{:S(2)}, u32[]{:S(2)}) async-start(bf16[8,3,16,2048]{3,2,1,0:T(8,128)(2,1)} %copy-done.2), calls=%async_computation.8 | async-start | bytes 3145728 | tf_op jit(solution)/shard_map/all_to_all | solution.py:7
  483.0 1.6 copy-start.4
  490.6 2.2 slice-start
  491.4 2.3 slice-start.1
  491.8 1.9 copy-start.14
  491.8 1.9 copy-start.16
  493.7 1.0 copy-start.18
  493.7 1.0 copy-start.20
  520.5 1.2 copy-start.1
Sparse Core Ops, SparseCore 0:
  70.6 68.9 all-gather.4
  141.4 70.0 all-gather.2
  277.1 23.0 reduce-scatter.6
  343.0 67.2 reduce-scatter.4
